TPU v7x, 32 devices: a whole 2x2x4 slice. The times are simulated.
32 devices in a mesh: region: 4 (over z), dom: 8 (over y, x, core).
Axes of the slice: x: 2, y: 2, z: 4, core: 2. Of those that a mesh axis runs over, the one named last changes fastest.
Arguments:
- fine_blocks: bfloat16 [1536, 7, 128, 128], P(('region', 'dom')), may hold values from -6 to 6
- interp: bfloat16 [1536, 8192], P(('region', 'dom')), may hold values from -0.5 to 0.5
- fine_cols: int32 [1536, 7], P(('region', 'dom')), may hold values from 0 to 1535, as said below
- fine_slot: int32 [1536, 7], P(('region', 'dom')), may hold values from 0 to 6
- fine_owner: int32 [1536, 1], P(('region', 'dom')), may hold values from 0 to 7; in each aligned block of 48 rows (0 to 47, 48 to 95, ...) at most 6 rows name the same one
- fine_place: int32 [1536], P(('region', 'dom')), may hold values from 0 to 23
- coarse_interp: bfloat16 [768, 2048], P(('region', 'dom')), may hold values from -0.75 to 0.75
- coarse_cols: int32 [768, 7], P(('region', 'dom')), may hold values from 0 to 767, as said below
- coarse_slot: int32 [768, 7], P(('region', 'dom')), may hold values from 0 to 6
- coarse_owner: int32 [768, 1], P(('region', 'dom')), may hold values from 0 to 7; in each aligned block of 24 rows (0 to 23, 24 to 47, ...) at most 3 rows name the same one
- coarse_place: int32 [768], P(('region', 'dom')), may hold values from 0 to 11
Outputs:
- coarse_blocks: bfloat16 [768, 7, 4096], P(('region', 'dom'))
- coarse2_blocks: bfloat16 [384, 7, 1024], P(('region', 'dom'))
Inputs may be any that keep to these rules, and one draw needn't show every extreme that they name: fine_cols[i, 0] = i; every other entry names a fine row held by the device of the same dom index in the same region or in an adjacent region. coarse_cols[q, 0] = q; every other entry names a coarse row of the same region or of an adjacent region. `fine_owner`: among the rows of one device, no owner is named more than 6 times, a bound that some block reaches. `coarse_owner`: among the rows of one device, no owner is named more than 3 times, a bound that some block reaches.
All inputs are finite; a program needn't handle non-finite values.
Results may differ from a plain program's by a relative error of at most 0.0065.
Values may be sent and summed in bfloat16 or wider, within the bound.
No kernel may reach another device: no remote copies, remote signals or barrier semaphores. Data moves between devices by JAX's collectives and lax.ppermute only.
A program may use at most 128 MiB of HBM per device.

v0:
```python
import jax
import jax.numpy as jnp
from jax import lax
from jax.sharding import PartitionSpec as P


def extended(cells, sides, width):
    for axis, dim in sides:
        count = lax.axis_size(axis)
        ends = count - 1
        head = lax.slice_in_dim(cells, 0, width, axis=dim)
        tail = lax.slice_in_dim(cells, cells.shape[dim] - width, cells.shape[dim], axis=dim)
        cells = jnp.concatenate(
            [
                lax.ppermute(tail, axis, [(i, (i + 1) % count) for i in range(ends)]),
                cells,
                lax.ppermute(head, axis, [((i + 1) % count, i) for i in range(ends)]),
            ],
            axis=dim,
        )
    return cells


def block_products(blocks, picked):
    return jnp.einsum("rkab,rkbc->rkac", blocks, picked, preferred_element_type=jnp.float32).astype(
        jnp.bfloat16
    )


def slot_table(slot, stencil):
    letters = jnp.arange(stencil, dtype=jnp.int32)
    return (slot[:, :, None] == letters[None, None, :]).astype(jnp.float32)


def restrict_terms(product, own_rows, choose):
    count = product.shape[0]
    stencil = product.shape[1]
    narrow = own_rows.shape[2]
    term = jnp.einsum("rac,rkad->rkcd", own_rows, product, preferred_element_type=jnp.float32)
    term = term.reshape(count, stencil, narrow * narrow)
    return jnp.einsum("rks,rkx->rsx", choose, term, precision=lax.Precision.HIGHEST)


def block_terms(blocks, picked, own_rows, slot):
    product = block_products(blocks, picked)
    return restrict_terms(product, own_rows, slot_table(slot, blocks.shape[1]))


def owner_positions(owner, parts, capacity):
    member = (owner[:, None] == jnp.arange(parts, dtype=jnp.int32)[None, :]).astype(jnp.int32)
    before = jnp.cumsum(member, axis=0) - member
    rank = jnp.sum(before * member, axis=1)
    return owner * capacity + rank


def place_into(values, position, slots):
    return jnp.zeros((slots,) + values.shape[1:], values.dtype).at[position].set(values)


def pack_owned(values, owner, place, parts, capacity, owned):
    position = owner_positions(owner, parts, capacity)
    buffer = place_into(values, position, parts * capacity)
    labels = (place[:, None] == jnp.arange(owned, dtype=jnp.int32)[None, :]).astype(jnp.float32)
    marks = place_into(labels, position, parts * capacity)
    return (buffer, marks)


def local(
    fine_blocks,
    interp,
    fine_cols,
    fine_slot,
    fine_owner,
    fine_place,
    coarse_interp,
    coarse_cols,
    coarse_slot,
    coarse_owner,
    coarse_place,
):
    rows = fine_blocks.shape[0]
    stencil = fine_blocks.shape[1]
    width = fine_blocks.shape[2]
    narrow = interp.shape[1] // width
    narrow2 = coarse_interp.shape[1] // narrow
    parts = lax.axis_size("dom")
    region = lax.axis_index("region")
    owned = rows // 2
    owned2 = owned // 2
    capacity = max(2, rows // 8)
    capacity2 = max(2, owned // 8)
    nearby_rows = extended(interp, (("region", 0),), rows)
    span = parts * rows
    index = (fine_cols // span - region + 1) * rows + fine_cols % rows
    picked = nearby_rows[index].reshape(rows, stencil, width, narrow)
    own_rows = interp.reshape(rows, width, narrow)
    slotted = block_terms(fine_blocks, picked, own_rows, fine_slot)
    sent, marks = pack_owned(slotted, fine_owner[:, 0], fine_place, parts, capacity, owned)
    arrived, labels = (
        lax.all_to_all(sent, "dom", split_axis=0, concat_axis=0, tiled=True),
        lax.all_to_all(marks, "dom", split_axis=0, concat_axis=0, tiled=True),
    )
    coarse_sum = jnp.einsum("rc,rkx->ckx", labels, arrived, precision=lax.Precision.HIGHEST)
    coarse_blocks = coarse_sum.astype(jnp.bfloat16)
    span2 = parts * owned
    flat = coarse_interp.shape[1]
    widened = extended(coarse_interp, (("region", 0),), owned)
    stacked = widened.reshape(3, owned, flat)
    collected = lax.all_gather(stacked, "dom", axis=1, tiled=True)
    table = collected.reshape(3 * span2, flat)
    index2 = (coarse_cols // span2 - region + 1) * span2 + coarse_cols % span2
    picked2 = table[index2].reshape(owned, stencil, narrow, narrow2)
    square = coarse_blocks.reshape(owned, stencil, narrow, narrow)
    own_coarse = coarse_interp.reshape(owned, narrow, narrow2)
    slotted2 = block_terms(square, picked2, own_coarse, coarse_slot)
    sent2, marks2 = pack_owned(slotted2, coarse_owner[:, 0], coarse_place, parts, capacity2, owned2)
    arrived2, labels2 = (
        lax.all_to_all(sent2, "dom", split_axis=0, concat_axis=0, tiled=True),
        lax.all_to_all(marks2, "dom", split_axis=0, concat_axis=0, tiled=True),
    )
    second_sum = jnp.einsum("rc,rkx->ckx", labels2, arrived2, precision=lax.Precision.HIGHEST)
    return (coarse_blocks, second_sum.astype(jnp.bfloat16))


def solution(mesh):
    in_specs = (
        P(("region", "dom"), None, None, None),
        P(("region", "dom"), None),
        P(("region", "dom"), None),
        P(("region", "dom"), None),
        P(("region", "dom"), None),
        P(("region", "dom")),
        P(("region", "dom"), None),
        P(("region", "dom"), None),
        P(("region", "dom"), None),
        P(("region", "dom"), None),
        P(("region", "dom")),
    )
    out_specs = (P(("region", "dom"), None, None), P(("region", "dom"), None, None))
    return jax.shard_map(local, mesh=mesh, in_specs=in_specs, out_specs=out_specs, check_vma=False)
```

profile of v0, /device:TPU:0, one launch (start us, length us, event | category | flops | bytes accessed | tf_op | source)
XLA Modules:
  0.0 265.8 jit_solution(9862358425277935994)
XLA Ops:
  7.2 5.0 %collective-permute-start = (bf16[48,8192]{1,0:T(8,128)(2,1)}, bf16[48,8192]{1,0:T(8,128)(2,1)S(1)}, u32[]{:S(2)}, u32[]{:S(2)}) collective-permute-start(bf16[48,8192]{1,0:T(8,128)(2,1)} %param.12), channel_id=1, source_target_pairs={{0,8},{8,16},{16,24},{1,9},{9,17},{17,25},{2,10},{10,18},{18,26},{... | collective-permute-start | bytes 2359304 | tf_op jit(solution)/shard_map/ppermute | solution.py:15
  12.2 1.3 collective-permute-start.1
  17.4 3.7 %all-to-all-start = ((f32[8,1,144]{2,1,0:T(1,128)}), f32[8,1,144]{2,1,0:T(1,128)S(1)}, u32[]{:S(2)}, u32[]{:S(2)}) async-start(f32[8,1,144]{2,1,0:T(1,128)} %reshape.114), calls=%async_computation | async-start | bytes 16384 | tf_op jit(solution)/shard_map/all_to_all | solution.py:101
  21.1 3.4 %reshape.42 = bf16[48,128,64]{2,1,0:T(8,128)(2,1)} reshape(bf16[48,8192]{1,0:T(8,128)(2,1)} %param.12) | data formatting | bytes 1572864 | tf_op jit(solution)/shard_map/reshape | solution.py:96
  26.2 3.0 %collective-permute-done = bf16[48,8192]{1,0:T(8,128)(2,1)S(1)} collective-permute-done((bf16[48,8192]{1,0:T(8,128)(2,1)}, bf16[48,8192]{1,0:T(8,128)(2,1)S(1)}, u32[]{:S(2)}, u32[]{:S(2)}) %collective-permute-start) | collective-permute-done | bytes 786464 | tf_op jit(solution)/shard_map/ppermute | solution.py:15
  29.2 4.2 %collective-permute-done.1 = bf16[48,8192]{1,0:T(8,128)(2,1)} collective-permute-done((bf16[48,8192]{1,0:T(8,128)(2,1)}, bf16[48,8192]{1,0:T(8,128)(2,1)}, u32[]{:S(2)}, u32[]{:S(2)}) %collective-permute-start.1) | collective-permute-done | bytes 786464 | tf_op jit(solution)/shard_map/ppermute | solution.py:17
  33.4 1.5 pad_maximum_fusion
  34.9 6.9 %gather_fusion = bf16[336,8192]{1,0:T(8,128)(2,1)} fusion(bf16[144,8192]{1,0:T(8,128)(2,1)S(1)} %pad_maximum_fusion, s32[1024]{0:T(1024)S(1)} %pad_clamp_fusion.1), kind=kCustom, calls=%fused_computation | custom fusion | bytes 11011392 | tf_op jit(solution)/shard_map/gather | solution.py:95
  41.8 16.0 %reshape.41 = bf16[48,7,128,64]{3,2,1,0:T(8,128)(2,1)} reshape(bf16[336,8192]{1,0:T(8,128)(2,1)} %gather_fusion) | data formatting | bytes 11010048 | tf_op jit(solution)/shard_map/reshape | solution.py:95
  57.9 16.6 %fusion.10 = f32[48,7,64,64]{2,3,1,0:T(8,128)} fusion(bf16[48,7,128,64]{3,2,1,0:T(8,128)(2,1)} %reshape.41, bf16[48,7,128,128]{3,2,1,0:T(8,128)(2,1)} %param.11, bf16[48,128,64]{2,1,0:T(8,128)(2,1)S(1)} %copy-done), kind=kOutput, calls=%fused_computation.13 | convolution fusion | flops 1059717120 | bytes 22806528 | tf_op jit(solution)/shard_map/rac,rkad->rkcd/dot_general | solution.py:39
  74.4 12.2 %copy.58 = f32[48,7,64,64]{3,2,1,0:T(8,128)} copy(f32[48,7,64,64]{2,3,1,0:T(8,128)} %fusion.10) | data formatting | bytes 11010048 | tf_op jit(solution)/shard_map/reshape | solution.py:40
  86.6 10.3 %reshape.108 = f32[48,7,4096]{2,1,0:T(8,128)} reshape(f32[48,7,64,64]{3,2,1,0:T(8,128)} %copy.58) | data formatting | bytes 11010048 | tf_op jit(solution)/shard_map/reshape | solution.py:40
  96.9 8.4 %fusion.23 = f32[48,7,4096]{2,1,0:T(8,128)} fusion(f32[48,7,4096]{2,1,0:T(8,128)} %reshape.108, s32[48,7]{1,0:T(8,128)S(1)} %copy.31), kind=kOutput, calls=%fused_computation.25 | convolution fusion | flops 115607856 | bytes 11011392 | tf_op jit(solution)/shard_map/rks,rkx->rsx/dot_general | solution.py:41
  105.3 3.4 %broadcast_in_dim.13 = f32[48,7,4096]{2,1,0:T(8,128)} broadcast(f32[]{:T(128)} %constant.30.clone.1), dimensions={} | broadcast | bytes 5505028 | tf_op jit(solution)/shard_map/broadcast_in_dim | solution.py:57
  108.7 12.3 %scatter_fusion = f32[48,7,4096]{2,1,0:T(8,128)} fusion(f32[48,7,4096]{2,1,0:T(8,128)} %broadcast_in_dim.13, s32[48]{0:T(128)S(1)} %fusion.49, f32[48,7,4096]{2,1,0:T(8,128)} %fusion.23), kind=kCustom, calls=%fused_computation.3 | custom fusion | bytes 16515264 | tf_op jit(solution)/shard_map/scatter | solution.py:57
  121.0 4.9 %all-to-all-start.1 = ((f32[48,7,4096]{2,1,0:T(8,128)}), f32[48,7,4096]{2,1,0:T(8,128)}, u32[]{:S(2)}, u32[]{:S(2)}) async-start(f32[48,7,4096]{2,1,0:T(8,128)} %scatter_fusion), calls=%async_computation.1 | async-start | bytes 12582912 | tf_op jit(solution)/shard_map/all_to_all | solution.py:100
  126.0 3.4 %collective-permute-start.2 = (bf16[24,2048]{1,0:T(8,128)(2,1)S(1)}, bf16[24,2048]{1,0:T(8,128)(2,1)S(1)}, u32[]{:S(2)}, u32[]{:S(2)}) collective-permute-start(bf16[24,2048]{1,0:T(8,128)(2,1)S(1)} %copy-done.2), channel_id=1, source_target_pairs={{0,8},{8,16},{16,24},{1,9},{9,17},{17,25},{2,10},{10,18},{18,26},{... | collective-permute-start | bytes 294920 | tf_op jit(solution)/shard_map/ppermute | solution.py:15
  129.4 1.5 collective-permute-start.3
  132.0 4.1 %collective-permute-done.3 = bf16[24,2048]{1,0:T(8,128)(2,1)S(1)} collective-permute-done((bf16[24,2048]{1,0:T(8,128)(2,1)S(1)}, bf16[24,2048]{1,0:T(8,128)(2,1)S(1)}, u32[]{:S(2)}, u32[]{:S(2)}) %collective-permute-start.3) | collective-permute-done | bytes 98336 | tf_op jit(solution)/shard_map/ppermute | solution.py:17
  141.8 48.3 %all-gather.2.cloned.1.call-done = bf16[3,192,2048]{2,1,0:T(8,128)(2,1)} async-done(((bf16[3,24,2048]{2,1,0:T(8,128)(2,1)}), bf16[3,192,2048]{2,1,0:T(8,128)(2,1)}) %all-gather.2.cloned.1.call-update) | async-done | bytes 2359312 | tf_op jit(solution)/shard_map/all_gather | solution.py:109
  190.1 3.7 %gather_fusion.1 = bf16[168,2048]{1,0:T(8,128)(2,1)S(1)} fusion(bf16[576,2048]{1,0:T(8,128)(2,1)} %bitcast.52, s32[1024]{0:T(1024)S(1)} %pad_clamp_fusion), kind=kCustom, calls=%fused_computation.1 | custom fusion | bytes 1376928 | tf_op jit(solution)/shard_map/gather | solution.py:112
  193.8 2.0 reshape.47
  195.8 11.2 %all-to-all-done.1 = f32[48,7,4096]{2,1,0:T(8,128)} async-done(((f32[48,7,4096]{2,1,0:T(8,128)}), f32[48,7,4096]{2,1,0:T(8,128)}, u32[]{:S(2)}, u32[]{:S(2)}) %all-to-all-start.1) | async-done | bytes 5505056 | tf_op jit(solution)/shard_map/all_to_all | solution.py:100
  207.0 3.3 %all-to-all-start.2 = ((f32[8,3,12]{2,1,0:T(4,128)}), f32[8,3,12]{2,1,0:T(4,128)S(1)}, u32[]{:S(2)}, u32[]{:S(2)}) async-start(f32[8,3,12]{2,1,0:T(4,128)} %all_to_all.26), calls=%async_computation.2 | async-start | bytes 32768 | tf_op jit(solution)/shard_map/all_to_all | solution.py:119
  210.3 9.4 %fusion.7 = bf16[24,7,4096]{2,0,1:T(8,128)(2,1)} fusion(f32[48,7,4096]{2,1,0:T(8,128)} %all-to-all-done.1, f32[48,24]{1,0:T(8,128)S(1)} %all_to_all.24), kind=kOutput, calls=%fused_computation.12 | convolution fusion | flops 397049856 | bytes 6885888 | tf_op jit(solution)/shard_map/rc,rkx->ckx/dot_general | solution.py:103
  219.7 5.0 %reshape.44 = bf16[24,7,64,64]{3,2,0,1:T(8,128)(2,1)} reshape(bf16[24,7,4096]{2,0,1:T(8,128)(2,1)} %fusion.7) | data formatting | bytes 2752512 | tf_op jit(solution)/shard_map/reshape | solution.py:113
  224.7 5.3 %convolution_bitcast_fusion = f32[24,7,32,32]{2,3,1,0:T(8,128)} fusion(bf16[24,7,64,32]{3,2,1,0:T(8,128)(2,1)S(1)} %reshape.47, bf16[24,7,64,64]{3,2,0,1:T(8,128)(2,1)} %reshape.44, bf16[24,64,32]{2,1,0:T(8,128)(2,1)S(1)} %copy-done.1), kind=kOutput, calls=%fused_computation.17 | convolution fusion | flops 66404352 | bytes 2850816 | tf_op jit(solution)/shard_map/rac,rkad->rkcd/dot_general | solution.py:39
  230.0 2.2 copy.62
  233.4 1.2 fusion.25
  235.6 4.9 %scatter_fusion.1 = f32[24,7,1024]{2,1,0:T(8,128)} fusion(f32[24,7,1024]{2,1,0:T(8,128)} %broadcast_in_dim.16, s32[24]{0:T(128)} %copy-done.6, f32[24,7,1024]{2,1,0:T(8,128)S(1)} %fusion.25), kind=kCustom, calls=%fused_computation.5 | custom fusion | bytes 2064480 | tf_op jit(solution)/shard_map/scatter | solution.py:57
  240.5 4.1 %all-to-all-start.3 = ((f32[24,7,1024]{2,1,0:T(8,128)}), f32[24,7,1024]{2,1,0:T(8,128)S(1)}, u32[]{:S(2)}, u32[]{:S(2)}) async-start(f32[24,7,1024]{2,1,0:T(8,128)} %scatter_fusion.1), calls=%async_computation.3 | async-start | bytes 1572864 | tf_op jit(solution)/shard_map/all_to_all | solution.py:118
  244.6 12.6 %all-to-all-done.3 = f32[24,7,1024]{2,1,0:T(8,128)S(1)} async-done(((f32[24,7,1024]{2,1,0:T(8,128)}), f32[24,7,1024]{2,1,0:T(8,128)S(1)}, u32[]{:S(2)}, u32[]{:S(2)}) %all-to-all-start.3) | async-done | bytes 688160 | tf_op jit(solution)/shard_map/all_to_all | solution.py:118
  (55 shorter events, 16.2 us)
Async XLA Ops:
  7.2 22.0 %collective-permute-start = (bf16[48,8192]{1,0:T(8,128)(2,1)}, bf16[48,8192]{1,0:T(8,128)(2,1)S(1)}, u32[]{:S(2)}, u32[]{:S(2)}) collective-permute-start(bf16[48,8192]{1,0:T(8,128)(2,1)} %param.12), channel_id=1, source_target_pairs={{0,8},{8,16},{16,24},{1,9},{9,17},{17,25},{2,10},{10,18},{18,26},{... | collective-permute-start | bytes 2359304 | tf_op jit(solution)/shard_map/ppermute | solution.py:15
  12.2 21.2 %collective-permute-start.1 = (bf16[48,8192]{1,0:T(8,128)(2,1)}, bf16[48,8192]{1,0:T(8,128)(2,1)}, u32[]{:S(2)}, u32[]{:S(2)}) collective-permute-start(bf16[48,8192]{1,0:T(8,128)(2,1)} %param.12), channel_id=1, source_target_pairs={{8,0},{16,8},{24,16},{9,1},{17,9},{25,17},{10,2},{18,10},{26,18},{... | collective-permute-start | bytes 2359304 | tf_op jit(solution)/shard_map/ppermute | solution.py:17
  17.4 103.7 %all-to-all-start = ((f32[8,1,144]{2,1,0:T(1,128)}), f32[8,1,144]{2,1,0:T(1,128)S(1)}, u32[]{:S(2)}, u32[]{:S(2)}) async-start(f32[8,1,144]{2,1,0:T(1,128)} %reshape.114), calls=%async_computation | async-start | bytes 16384 | tf_op jit(solution)/shard_map/all_to_all | solution.py:101
  41.8 16.0 %copy-start = (bf16[48,128,64]{2,1,0:T(8,128)(2,1)S(1)}, bf16[48,128,64]{2,1,0:T(8,128)(2,1)}, u32[]{:S(2)}) copy-start(bf16[48,128,64]{2,1,0:T(8,128)(2,1)} %reshape.42) | copy-start | bytes 2359300
  121.0 5.0 %copy-start.2 = (bf16[24,2048]{1,0:T(8,128)(2,1)S(1)}, bf16[24,2048]{1,0:T(8,128)(2,1)}, u32[]{:S(2)}) copy-start(bf16[24,2048]{1,0:T(8,128)(2,1)} %param.17) | copy-start | bytes 294916
  121.0 16.8 %copy-start.3 = (s32[24,7]{0,1:T(8,128)S(1)}, s32[24,7]{0,1:T(8,128)}, u32[]{:S(2)}) copy-start(s32[24,7]{0,1:T(8,128)} %param.18) | copy-start | bytes 2020
  121.0 17.0 %copy-start.4 = (s32[24,7]{0,1:T(8,128)S(1)}, s32[24,7]{0,1:T(8,128)}, u32[]{:S(2)}) copy-start(s32[24,7]{0,1:T(8,128)} %param.19) | copy-start | bytes 2020
  121.0 17.7 %copy-start.5 = (s32[24,1]{0,1:T(1,128)S(1)}, s32[24,1]{0,1:T(1,128)}, u32[]{:S(2)}) copy-start(s32[24,1]{0,1:T(1,128)} %param.20) | copy-start | bytes 292
  121.0 18.0 %copy-start.7 = (s32[24]{0:T(128)S(1)}, s32[24]{0:T(128)}, u32[]{:S(2)}) copy-start(s32[24]{0:T(128)} %param.21) | copy-start | bytes 292
  121.0 85.9 %all-to-all-start.1 = ((f32[48,7,4096]{2,1,0:T(8,128)}), f32[48,7,4096]{2,1,0:T(8,128)}, u32[]{:S(2)}, u32[]{:S(2)}) async-start(f32[48,7,4096]{2,1,0:T(8,128)} %scatter_fusion), calls=%async_computation.1 | async-start | bytes 12582912 | tf_op jit(solution)/shard_map/all_to_all | solution.py:100
  125.9 64.2 %all-gather.2.cloned.1.call-start = ((), (), s32[]{:S(2)}) async-start(), calls=%async_computation.4 | async-start | bytes 2654208 | tf_op jit(solution)/shard_map/all_gather | solution.py:109
  126.0 6.0 %collective-permute-start.2 = (bf16[24,2048]{1,0:T(8,128)(2,1)S(1)}, bf16[24,2048]{1,0:T(8,128)(2,1)S(1)}, u32[]{:S(2)}, u32[]{:S(2)}) collective-permute-start(bf16[24,2048]{1,0:T(8,128)(2,1)S(1)} %copy-done.2), channel_id=1, source_target_pairs={{0,8},{8,16},{16,24},{1,9},{9,17},{17,25},{2,10},{10,18},{18,26},{... | collective-permute-start | bytes 294920 | tf_op jit(solution)/shard_map/ppermute | solution.py:15
  129.4 6.6 %collective-permute-start.3 = (bf16[24,2048]{1,0:T(8,128)(2,1)S(1)}, bf16[24,2048]{1,0:T(8,128)(2,1)S(1)}, u32[]{:S(2)}, u32[]{:S(2)}) collective-permute-start(bf16[24,2048]{1,0:T(8,128)(2,1)S(1)} %copy-done.2), channel_id=1, source_target_pairs={{8,0},{16,8},{24,16},{9,1},{17,9},{25,17},{10,2},{18,10},{26,18},{... | collective-permute-start | bytes 294920 | tf_op jit(solution)/shard_map/ppermute | solution.py:17
  139.1 1.9 copy-start.6
  207.0 33.5 %all-to-all-start.2 = ((f32[8,3,12]{2,1,0:T(4,128)}), f32[8,3,12]{2,1,0:T(4,128)S(1)}, u32[]{:S(2)}, u32[]{:S(2)}) async-start(f32[8,3,12]{2,1,0:T(4,128)} %all_to_all.26), calls=%async_computation.2 | async-start | bytes 32768 | tf_op jit(solution)/shard_map/all_to_all | solution.py:119
  210.3 14.4 %copy-start.1 = (bf16[24,64,32]{2,1,0:T(8,128)(2,1)S(1)}, bf16[24,64,32]{2,1,0:T(8,128)(2,1)}, u32[]{:S(2)}) copy-start(bf16[24,64,32]{2,1,0:T(8,128)(2,1)} %reshape.48) | copy-start | bytes 294916
  240.5 16.7 %all-to-all-start.3 = ((f32[24,7,1024]{2,1,0:T(8,128)}), f32[24,7,1024]{2,1,0:T(8,128)S(1)}, u32[]{:S(2)}, u32[]{:S(2)}) async-start(f32[24,7,1024]{2,1,0:T(8,128)} %scatter_fusion.1), calls=%async_computation.3 | async-start | bytes 1572864 | tf_op jit(solution)/shard_map/all_to_all | solution.py:118
Sparse Core Ops, SparseCore 0:
  137.0 53.0 all-gather.1
where the time goes:
time: 268 us; the launch traced here: 266 us
  local copies, waits for them, and re-layouts  90.1 us (34%)
  waiting for transfers between devices  84.4 us (31%)
  matrix products  41.8 us (16%)
  starting transfers between devices  27.3 us (10%)
  between operations  14.2 us (5%)
  other arithmetic  7.92 us (3%)
    all_gather x1, waiting for transfers between devices, local(): collected = lax.all_gather(stacked, 'dom', axis=1, tiled=True)  48.3 us
    reshape x4, local copies, waits for them, and re-layouts, restrict_terms(): term = term.reshape(count, stencil, narrow * narrow)  25.8 us
    dot_general x2, matrix products, restrict_terms(): jnp.einsum('rac,rkad->rkcd', own_rows, product, preferred_element_type=jn...  21.9 us
    scatter x2, local copies, waits for them, and re-layouts, place_into(): jnp.zeros((slots,) + values.shape[1:], values.dtype).at[position]  17.2 us
    reshape x1, local copies, waits for them, and re-layouts, local(): picked = nearby_rows[index].reshape(rows, stencil, width, narrow)  16 us
    all_to_all x1, waiting for transfers between devices, local(): lax.all_to_all(sent2, 'dom', split_axis=0, concat_axis=0, tiled=True)  12.6 us
    all_to_all x1, waiting for transfers between devices, local(): lax.all_to_all(sent, 'dom', split_axis=0, concat_axis=0, tiled=True)  11.2 us
    dot_general x2, matrix products, restrict_terms(): jnp.einsum('rks,rkx->rsx', choose, term, precision=lax.Precision.HIGHEST)  9.63 us
  transfers between devices with their start and end apart: 9, of which 7 were waited for; matrix products, arithmetic and copies ran while one was open for 52% of the time, Pallas kernels for 0%

commit v1 on v0

--- a/solution.py
+++ b/solution.py
@@ -2,6 +2,24 @@
 import jax.numpy as jnp
 from jax import lax
 from jax.sharding import PartitionSpec as P
+
+
+def gather_around(value, axis, dim):
+    ways, here, lap = (lax.axis_size(axis), lax.axis_index(axis), value.shape[dim])
+    shape = [n * ways if d == dim else n for d, n in enumerate(value.shape)]
+    full = lax.dynamic_update_slice_in_dim(
+        jnp.zeros(shape, value.dtype), value, here * lap, axis=dim
+    )
+    going_up = going_down = value
+    for far in range(1, ways // 2 + 1):
+        going_up = lax.ppermute(going_up, axis, [(d, (d + 1) % ways) for d in range(ways)])
+        full = lax.dynamic_update_slice_in_dim(full, going_up, (here - far) % ways * lap, axis=dim)
+        if 2 * far < ways:
+            going_down = lax.ppermute(going_down, axis, [(d, (d - 1) % ways) for d in range(ways)])
+            full = lax.dynamic_update_slice_in_dim(
+                full, going_down, (here + far) % ways * lap, axis=dim
+            )
+    return full
 
 
 def extended(cells, sides, width):
@@ -106,7 +124,7 @@
     flat = coarse_interp.shape[1]
     widened = extended(coarse_interp, (("region", 0),), owned)
     stacked = widened.reshape(3, owned, flat)
-    collected = lax.all_gather(stacked, "dom", axis=1, tiled=True)
+    collected = gather_around(stacked, "dom", 1)
     table = collected.reshape(3 * span2, flat)
     index2 = (coarse_cols // span2 - region + 1) * span2 + coarse_cols % span2
     picked2 = table[index2].reshape(owned, stencil, narrow, narrow2)

time: 268 us -> 281 us (1.049)
  waiting for transfers between devices: 84.4 us -> 105 us
  between operations: 14.2 us -> 1.08 us
  starting transfers between devices: 27.3 us -> 35.4 us
    ppermute x0 -> x7, waiting for transfers between devices: none -> 84.1 us  [the longest x4 84.1 us: gather_around(): lax.ppermute(going_up, axis, [(d, (d + 1) % ways) for d in range(ways)])]
    all_gather x1 -> x0, waiting for transfers between devices: 48.3 us -> none  [local(): collected = lax.all_gather(stacked, 'dom', axis=1, tiled=True)]
    all_to_all x1, waiting for transfers between devices: 11.2 us -> 0.01 us  [local(): lax.all_to_all(sent, 'dom', split_axis=0, concat_axis=0, tiled=True)]
    ppermute x0 -> x7, starting transfers between devices: none -> 7.98 us  [the longest x3 7.92 us: gather_around(): lax.ppermute(going_down, axis, [(d, (d - 1) % ways) for d in range(ways)])]
    ppermute x2, waiting for transfers between devices: 8.28 us -> 4.94 us  [extended(): lax.ppermute(head, axis, [((i + 1) % count, i) for i in range(ends)])]
  transfers between devices with their start and end apart: 9 -> 15, of which waited for: 7 -> 8; matrix products, arithmetic and copies ran while one was open for 52% -> 48% of each run, Pallas kernels for 0% -> 0%
where the time goes in v1:
time: 281 us; the launch traced here: 279 us
  waiting for transfers between devices  105 us (37%)
  local copies, waits for them, and re-layouts  88.8 us (32%)
  matrix products  41.8 us (15%)
  starting transfers between devices  35.4 us (13%)
  other arithmetic  7.17 us (3%)
    ppermute x4, waiting for transfers between devices, gather_around(): lax.ppermute(going_up, axis, [(d, (d + 1) % ways) for d in range(ways)])  84.1 us
    reshape x4, local copies, waits for them, and re-layouts, restrict_terms(): term = term.reshape(count, stencil, narrow * narrow)  25.8 us
    dot_general x2, matrix products, restrict_terms(): jnp.einsum('rac,rkad->rkcd', own_rows, product, preferred_element_type=jn...  21.9 us
    scatter x2, local copies, waits for them, and re-layouts, place_into(): jnp.zeros((slots,) + values.shape[1:], values.dtype).at[position]  17.2 us
    reshape x1, local copies, waits for them, and re-layouts, local(): picked = nearby_rows[index].reshape(rows, stencil, width, narrow)  16 us
    all_to_all x1, waiting for transfers between devices, local(): lax.all_to_all(sent2, 'dom', split_axis=0, concat_axis=0, tiled=True)  12.6 us
    dot_general x2, matrix products, restrict_terms(): jnp.einsum('rks,rkx->rsx', choose, term, precision=lax.Precision.HIGHEST)  9.64 us
    dot_general x1, matrix products, local(): jnp.einsum('rc,rkx->ckx', labels, arrived, precision=lax.Precision.HIGHEST)  9.33 us
  transfers between devices with their start and end apart: 15, of which 8 were waited for; matrix products, arithmetic and copies ran while one was open for 48% of the time, Pallas kernels for 0%

profile of v1, /device:TPU:0, one launch (start us, length us, event | category | flops | bytes accessed | tf_op | source)
XLA Modules:
  0.0 278.9 jit_solution(10495383827097356005)
XLA Ops:
  0.6 5.1 %collective-permute-start = (bf16[48,8192]{1,0:T(8,128)(2,1)}, bf16[48,8192]{1,0:T(8,128)(2,1)S(1)}, u32[]{:S(2)}, u32[]{:S(2)}) collective-permute-start(bf16[48,8192]{1,0:T(8,128)(2,1)} %param.12), channel_id=1, source_target_pairs={{0,8},{8,16},{16,24},{1,9},{9,17},{17,25},{2,10},{10,18},{18,26},{... | collective-permute-start | bytes 2359304 | tf_op jit(solution)/shard_map/ppermute | solution.py:33
  11.0 3.7 %all-to-all-start = ((f32[8,1,144]{2,1,0:T(1,128)}), f32[8,1,144]{2,1,0:T(1,128)S(1)}, u32[]{:S(2)}, u32[]{:S(2)}) async-start(f32[8,1,144]{2,1,0:T(1,128)} %reshape.114), calls=%async_computation | async-start | bytes 16384 | tf_op jit(solution)/shard_map/all_to_all | solution.py:119
  14.7 3.4 %reshape.42 = bf16[48,128,64]{2,1,0:T(8,128)(2,1)} reshape(bf16[48,8192]{1,0:T(8,128)(2,1)} %param.12) | data formatting | bytes 1572864 | tf_op jit(solution)/shard_map/reshape | solution.py:114
  19.8 3.0 %collective-permute-done = bf16[48,8192]{1,0:T(8,128)(2,1)S(1)} collective-permute-done((bf16[48,8192]{1,0:T(8,128)(2,1)}, bf16[48,8192]{1,0:T(8,128)(2,1)S(1)}, u32[]{:S(2)}, u32[]{:S(2)}) %collective-permute-start) | collective-permute-done | bytes 786464 | tf_op jit(solution)/shard_map/ppermute | solution.py:33
  23.7 3.3 %collective-permute-done.1 = bf16[48,8192]{1,0:T(8,128)(2,1)} collective-permute-done((bf16[48,8192]{1,0:T(8,128)(2,1)}, bf16[48,8192]{1,0:T(8,128)(2,1)}, u32[]{:S(2)}, u32[]{:S(2)}) %collective-permute-start.1) | collective-permute-done | bytes 786464 | tf_op jit(solution)/shard_map/ppermute | solution.py:35
  28.5 6.9 %gather_fusion = bf16[336,8192]{1,0:T(8,128)(2,1)} fusion(bf16[144,8192]{1,0:T(8,128)(2,1)S(1)} %pad_maximum_fusion, s32[1024]{0:T(1024)S(1)} %pad_clamp_fusion.1), kind=kCustom, calls=%fused_computation | custom fusion | bytes 11011392 | tf_op jit(solution)/shard_map/gather | solution.py:113
  35.4 16.0 %reshape.41 = bf16[48,7,128,64]{3,2,1,0:T(8,128)(2,1)} reshape(bf16[336,8192]{1,0:T(8,128)(2,1)} %gather_fusion) | data formatting | bytes 11010048 | tf_op jit(solution)/shard_map/reshape | solution.py:113
  51.5 16.5 %fusion.10 = f32[48,7,64,64]{2,3,1,0:T(8,128)} fusion(bf16[48,7,128,64]{3,2,1,0:T(8,128)(2,1)} %reshape.41, bf16[48,7,128,128]{3,2,1,0:T(8,128)(2,1)} %param.11, bf16[48,128,64]{2,1,0:T(8,128)(2,1)S(1)} %copy-done), kind=kOutput, calls=%fused_computation.13 | convolution fusion | flops 1059717120 | bytes 22806528 | tf_op jit(solution)/shard_map/rac,rkad->rkcd/dot_general | solution.py:57
  68.0 12.2 %copy.58 = f32[48,7,64,64]{3,2,1,0:T(8,128)} copy(f32[48,7,64,64]{2,3,1,0:T(8,128)} %fusion.10) | data formatting | bytes 11010048 | tf_op jit(solution)/shard_map/reshape | solution.py:58
  80.2 10.3 %reshape.108 = f32[48,7,4096]{2,1,0:T(8,128)} reshape(f32[48,7,64,64]{3,2,1,0:T(8,128)} %copy.58) | data formatting | bytes 11010048 | tf_op jit(solution)/shard_map/reshape | solution.py:58
  90.4 8.4 %fusion.23 = f32[48,7,4096]{2,1,0:T(8,128)} fusion(f32[48,7,4096]{2,1,0:T(8,128)} %reshape.108, s32[48,7]{1,0:T(8,128)S(1)} %copy.31), kind=kOutput, calls=%fused_computation.25 | convolution fusion | flops 115607856 | bytes 11011392 | tf_op jit(solution)/shard_map/rks,rkx->rsx/dot_general | solution.py:59
  98.9 3.4 %broadcast_in_dim.15 = f32[48,7,4096]{2,1,0:T(8,128)} broadcast(f32[]{:T(128)} %constant.110.clone.1), dimensions={} | broadcast | bytes 5505028 | tf_op jit(solution)/shard_map/broadcast_in_dim | solution.py:75
  102.3 12.2 %scatter_fusion = f32[48,7,4096]{2,1,0:T(8,128)} fusion(f32[48,7,4096]{2,1,0:T(8,128)} %broadcast_in_dim.15, s32[48]{0:T(128)S(1)} %fusion.49, f32[48,7,4096]{2,1,0:T(8,128)} %fusion.23), kind=kCustom, calls=%fused_computation.3 | custom fusion | bytes 16515264 | tf_op jit(solution)/shard_map/scatter | solution.py:75
  114.5 5.1 %all-to-all-start.1 = ((f32[48,7,4096]{2,1,0:T(8,128)}), f32[48,7,4096]{2,1,0:T(8,128)}, u32[]{:S(2)}, u32[]{:S(2)}) async-start(f32[48,7,4096]{2,1,0:T(8,128)} %scatter_fusion), calls=%async_computation.1 | async-start | bytes 12582912 | tf_op jit(solution)/shard_map/all_to_all | solution.py:118
  119.6 3.5 %collective-permute-start.2 = (bf16[24,2048]{1,0:T(8,128)(2,1)S(1)}, bf16[24,2048]{1,0:T(8,128)(2,1)S(1)}, u32[]{:S(2)}, u32[]{:S(2)}) collective-permute-start(bf16[24,2048]{1,0:T(8,128)(2,1)S(1)} %copy-done.4), channel_id=1, source_target_pairs={{0,8},{8,16},{16,24},{1,9},{9,17},{17,25},{2,10},{10,18},{18,26},{... | collective-permute-start | bytes 294920 | tf_op jit(solution)/shard_map/ppermute | solution.py:33
  128.1 1.6 collective-permute-done.3
  129.9 2.6 collective-permute-start.5
  134.1 62.8 %collective-permute-done.4 = bf16[3,24,2048]{2,1,0:T(8,128)(2,1)S(1)} collective-permute-done((bf16[3,24,2048]{2,1,0:T(8,128)(2,1)S(1)}, bf16[3,24,2048]{2,1,0:T(8,128)(2,1)S(1)}, u32[]{:S(2)}, u32[]{:S(2)}) %collective-permute-start.4) | collective-permute-done | bytes 294944 | tf_op jit(solution)/shard_map/ppermute | solution.py:15
  197.0 2.6 collective-permute-start.7
  199.7 7.5 %collective-permute-done.6 = bf16[3,24,2048]{2,1,0:T(8,128)(2,1)S(1)} collective-permute-done((bf16[3,24,2048]{2,1,0:T(8,128)(2,1)S(1)}, bf16[3,24,2048]{2,1,0:T(8,128)(2,1)S(1)}, u32[]{:S(2)}, u32[]{:S(2)}) %collective-permute-start.6) | collective-permute-done | bytes 294944 | tf_op jit(solution)/shard_map/ppermute | solution.py:15
  207.2 2.6 collective-permute-start.9
  209.9 6.8 %collective-permute-done.8 = bf16[3,24,2048]{2,1,0:T(8,128)(2,1)S(1)} collective-permute-done((bf16[3,24,2048]{2,1,0:T(8,128)(2,1)S(1)}, bf16[3,24,2048]{2,1,0:T(8,128)(2,1)S(1)}, u32[]{:S(2)}, u32[]{:S(2)}) %collective-permute-start.8) | collective-permute-done | bytes 294944 | tf_op jit(solution)/shard_map/ppermute | solution.py:15
  216.8 7.0 %collective-permute-done.10 = bf16[3,24,2048]{2,1,0:T(8,128)(2,1)S(1)} collective-permute-done((bf16[3,24,2048]{2,1,0:T(8,128)(2,1)S(1)}, bf16[3,24,2048]{2,1,0:T(8,128)(2,1)S(1)}, u32[]{:S(2)}, u32[]{:S(2)}) %collective-permute-start.10) | collective-permute-done | bytes 294944 | tf_op jit(solution)/shard_map/ppermute | solution.py:15
  224.9 2.0 reshape.47
  226.9 3.3 %all-to-all-start.2 = ((f32[8,3,12]{2,1,0:T(4,128)}), f32[8,3,12]{2,1,0:T(4,128)S(1)}, u32[]{:S(2)}, u32[]{:S(2)}) async-start(f32[8,3,12]{2,1,0:T(4,128)} %all_to_all.26), calls=%async_computation.2 | async-start | bytes 32768 | tf_op jit(solution)/shard_map/all_to_all | solution.py:137
  230.2 9.3 %fusion.7 = bf16[24,7,4096]{2,0,1:T(8,128)(2,1)} fusion(f32[48,7,4096]{2,1,0:T(8,128)} %all-to-all-done.1, f32[48,24]{1,0:T(8,128)S(1)} %all_to_all.24), kind=kOutput, calls=%fused_computation.12 | convolution fusion | flops 397049856 | bytes 6885888 | tf_op jit(solution)/shard_map/rc,rkx->ckx/dot_general | solution.py:121
  239.6 5.0 %reshape.44 = bf16[24,7,64,64]{3,2,0,1:T(8,128)(2,1)} reshape(bf16[24,7,4096]{2,0,1:T(8,128)(2,1)} %fusion.7) | data formatting | bytes 2752512 | tf_op jit(solution)/shard_map/reshape | solution.py:131
  244.6 5.3 %convolution_bitcast_fusion = f32[24,7,32,32]{2,3,1,0:T(8,128)} fusion(bf16[24,7,64,32]{3,2,1,0:T(8,128)(2,1)S(1)} %reshape.47, bf16[24,7,64,64]{3,2,0,1:T(8,128)(2,1)} %reshape.44, bf16[24,64,32]{2,1,0:T(8,128)(2,1)S(1)} %copy-done.2), kind=kOutput, calls=%fused_computation.17 | convolution fusion | flops 66404352 | bytes 2850816 | tf_op jit(solution)/shard_map/rac,rkad->rkcd/dot_general | solution.py:57
  249.9 2.2 copy.62
  255.5 5.0 %scatter_fusion.1 = f32[24,7,1024]{2,1,0:T(8,128)} fusion(f32[24,7,1024]{2,1,0:T(8,128)} %broadcast_in_dim.18, s32[24]{0:T(128)} %copy-done.8, f32[24,7,1024]{2,1,0:T(8,128)S(1)} %fusion.25), kind=kCustom, calls=%fused_computation.5 | custom fusion | bytes 2064480 | tf_op jit(solution)/shard_map/scatter | solution.py:75
  260.5 4.1 %all-to-all-start.3 = ((f32[24,7,1024]{2,1,0:T(8,128)}), f32[24,7,1024]{2,1,0:T(8,128)S(1)}, u32[]{:S(2)}, u32[]{:S(2)}) async-start(f32[24,7,1024]{2,1,0:T(8,128)} %scatter_fusion.1), calls=%async_computation.3 | async-start | bytes 1572864 | tf_op jit(solution)/shard_map/all_to_all | solution.py:136
  264.6 12.6 %all-to-all-done.3 = f32[24,7,1024]{2,1,0:T(8,128)S(1)} async-done(((f32[24,7,1024]{2,1,0:T(8,128)}), f32[24,7,1024]{2,1,0:T(8,128)S(1)}, u32[]{:S(2)}, u32[]{:S(2)}) %all-to-all-start.3) | async-done | bytes 688160 | tf_op jit(solution)/shard_map/all_to_all | solution.py:136
  (79 shorter events, 22.1 us)
Async XLA Ops:
  0.6 26.3 %copy-start.1 = (bf16[48,8192]{1,0:T(8,128)(2,1)S(1)}, bf16[48,8192]{1,0:T(8,128)(2,1)}, u32[]{:S(2)}) copy-start(bf16[48,8192]{1,0:T(8,128)(2,1)} %param.12) | copy-start | bytes 2359300
  0.6 22.2 %collective-permute-start = (bf16[48,8192]{1,0:T(8,128)(2,1)}, bf16[48,8192]{1,0:T(8,128)(2,1)S(1)}, u32[]{:S(2)}, u32[]{:S(2)}) collective-permute-start(bf16[48,8192]{1,0:T(8,128)(2,1)} %param.12), channel_id=1, source_target_pairs={{0,8},{8,16},{16,24},{1,9},{9,17},{17,25},{2,10},{10,18},{18,26},{... | collective-permute-start | bytes 2359304 | tf_op jit(solution)/shard_map/ppermute | solution.py:33
  5.8 21.2 %collective-permute-start.1 = (bf16[48,8192]{1,0:T(8,128)(2,1)}, bf16[48,8192]{1,0:T(8,128)(2,1)}, u32[]{:S(2)}, u32[]{:S(2)}) collective-permute-start(bf16[48,8192]{1,0:T(8,128)(2,1)} %param.12), channel_id=1, source_target_pairs={{8,0},{16,8},{24,16},{9,1},{17,9},{25,17},{10,2},{18,10},{26,18},{... | collective-permute-start | bytes 2359304 | tf_op jit(solution)/shard_map/ppermute | solution.py:35
  11.0 103.5 %all-to-all-start = ((f32[8,1,144]{2,1,0:T(1,128)}), f32[8,1,144]{2,1,0:T(1,128)S(1)}, u32[]{:S(2)}, u32[]{:S(2)}) async-start(f32[8,1,144]{2,1,0:T(1,128)} %reshape.114), calls=%async_computation | async-start | bytes 16384 | tf_op jit(solution)/shard_map/all_to_all | solution.py:119
  22.8 0.9 copy-start.3
  35.4 16.0 %copy-start = (bf16[48,128,64]{2,1,0:T(8,128)(2,1)S(1)}, bf16[48,128,64]{2,1,0:T(8,128)(2,1)}, u32[]{:S(2)}) copy-start(bf16[48,128,64]{2,1,0:T(8,128)(2,1)} %reshape.42) | copy-start | bytes 2359300
  114.5 5.1 %copy-start.4 = (bf16[24,2048]{1,0:T(8,128)(2,1)S(1)}, bf16[24,2048]{1,0:T(8,128)(2,1)}, u32[]{:S(2)}) copy-start(bf16[24,2048]{1,0:T(8,128)(2,1)} %param.17) | copy-start | bytes 294916
  114.5 9.9 %copy-start.7 = (s32[24,1]{0,1:T(1,128)S(1)}, s32[24,1]{0,1:T(1,128)}, u32[]{:S(2)}) copy-start(s32[24,1]{0,1:T(1,128)} %param.20) | copy-start | bytes 292
  114.5 10.2 %copy-start.5 = (s32[24,7]{0,1:T(8,128)S(1)}, s32[24,7]{0,1:T(8,128)}, u32[]{:S(2)}) copy-start(s32[24,7]{0,1:T(8,128)} %param.18) | copy-start | bytes 2020
  114.5 11.6 %copy-start.6 = (s32[24,7]{0,1:T(8,128)S(1)}, s32[24,7]{0,1:T(8,128)}, u32[]{:S(2)}) copy-start(s32[24,7]{0,1:T(8,128)} %param.19) | copy-start | bytes 2020
  114.5 12.3 %copy-start.9 = (s32[24]{0:T(128)S(1)}, s32[24]{0:T(128)}, u32[]{:S(2)}) copy-start(s32[24]{0:T(128)} %param.21) | copy-start | bytes 292
  114.5 112.3 %all-to-all-start.1 = ((f32[48,7,4096]{2,1,0:T(8,128)}), f32[48,7,4096]{2,1,0:T(8,128)}, u32[]{:S(2)}, u32[]{:S(2)}) async-start(f32[48,7,4096]{2,1,0:T(8,128)} %scatter_fusion), calls=%async_computation.1 | async-start | bytes 12582912 | tf_op jit(solution)/shard_map/all_to_all | solution.py:118
  119.6 8.5 %collective-permute-start.2 = (bf16[24,2048]{1,0:T(8,128)(2,1)S(1)}, bf16[24,2048]{1,0:T(8,128)(2,1)S(1)}, u32[]{:S(2)}, u32[]{:S(2)}) collective-permute-start(bf16[24,2048]{1,0:T(8,128)(2,1)S(1)} %copy-done.4), channel_id=1, source_target_pairs={{0,8},{8,16},{16,24},{1,9},{9,17},{17,25},{2,10},{10,18},{18,26},{... | collective-permute-start | bytes 294920 | tf_op jit(solution)/shard_map/ppermute | solution.py:33
  123.1 6.7 %collective-permute-start.3 = (bf16[24,2048]{1,0:T(8,128)(2,1)S(1)}, bf16[24,2048]{1,0:T(8,128)(2,1)S(1)}, u32[]{:S(2)}, u32[]{:S(2)}) collective-permute-start(bf16[24,2048]{1,0:T(8,128)(2,1)S(1)} %copy-done.4), channel_id=1, source_target_pairs={{8,0},{16,8},{24,16},{9,1},{17,9},{25,17},{10,2},{18,10},{26,18},{... | collective-permute-start | bytes 294920 | tf_op jit(solution)/shard_map/ppermute | solution.py:35
  124.8 7.7 %copy-start.8 = (s32[24]{0:T(128)}, s32[24]{0:T(128)S(1)}, u32[]{:S(2)}) copy-start(s32[24]{0:T(128)S(1)} %fusion.50) | copy-start | bytes 292
  129.8 67.1 %collective-permute-start.4 = (bf16[3,24,2048]{2,1,0:T(8,128)(2,1)S(1)}, bf16[3,24,2048]{2,1,0:T(8,128)(2,1)S(1)}, u32[]{:S(2)}, u32[]{:S(2)}) collective-permute-start(bf16[3,24,2048]{2,1,0:T(8,128)(2,1)S(1)} %bitcast.53), channel_id=1, source_target_pairs={{0,1},{1,2},{2,3},{3,4},{4,5},{5,6},{6,7},{7,0},{8,9},{9,10},{10,1... | collective-permute-start | bytes 884744 | tf_op jit(solution)/shard_map/ppermute | solution.py:15
  129.9 67.1 %collective-permute-start.5 = (bf16[3,24,2048]{2,1,0:T(8,128)(2,1)S(1)}, bf16[3,24,2048]{2,1,0:T(8,128)(2,1)S(1)}, u32[]{:S(2)}, u32[]{:S(2)}) collective-permute-start(bf16[3,24,2048]{2,1,0:T(8,128)(2,1)S(1)} %bitcast.54), channel_id=1, source_target_pairs={{0,7},{1,0},{2,1},{3,2},{4,3},{5,4},{6,5},{7,6},{8,15},{9,8},{10,9... | collective-permute-start | bytes 884744 | tf_op jit(solution)/shard_map/ppermute | solution.py:18
  197.0 10.2 %collective-permute-start.6 = (bf16[3,24,2048]{2,1,0:T(8,128)(2,1)S(1)}, bf16[3,24,2048]{2,1,0:T(8,128)(2,1)S(1)}, u32[]{:S(2)}, u32[]{:S(2)}) collective-permute-start(bf16[3,24,2048]{2,1,0:T(8,128)(2,1)S(1)} %collective-permute-done.4), channel_id=1, source_target_pairs={{0,1},{1,2},{2,3},{3,4},{4,5},{5,6},{6,7},{7,0},{8,9},{9,10},{10,1... | collective-permute-start | bytes 884744 | tf_op jit(solution)/shard_map/ppermute | solution.py:15
  197.0 10.2 %collective-permute-start.7 = (bf16[3,24,2048]{2,1,0:T(8,128)(2,1)S(1)}, bf16[3,24,2048]{2,1,0:T(8,128)(2,1)S(1)}, u32[]{:S(2)}, u32[]{:S(2)}) collective-permute-start(bf16[3,24,2048]{2,1,0:T(8,128)(2,1)S(1)} %collective-permute-done.5), channel_id=1, source_target_pairs={{0,7},{1,0},{2,1},{3,2},{4,3},{5,4},{6,5},{7,6},{8,15},{9,8},{10,9... | collective-permute-start | bytes 884744 | tf_op jit(solution)/shard_map/ppermute | solution.py:18
  207.1 9.5 %collective-permute-start.8 = (bf16[3,24,2048]{2,1,0:T(8,128)(2,1)S(1)}, bf16[3,24,2048]{2,1,0:T(8,128)(2,1)S(1)}, u32[]{:S(2)}, u32[]{:S(2)}) collective-permute-start(bf16[3,24,2048]{2,1,0:T(8,128)(2,1)S(1)} %collective-permute-done.6), channel_id=1, source_target_pairs={{0,1},{1,2},{2,3},{3,4},{4,5},{5,6},{6,7},{7,0},{8,9},{9,10},{10,1... | collective-permute-start | bytes 884744 | tf_op jit(solution)/shard_map/ppermute | solution.py:15
  207.2 9.6 %collective-permute-start.9 = (bf16[3,24,2048]{2,1,0:T(8,128)(2,1)S(1)}, bf16[3,24,2048]{2,1,0:T(8,128)(2,1)S(1)}, u32[]{:S(2)}, u32[]{:S(2)}) collective-permute-start(bf16[3,24,2048]{2,1,0:T(8,128)(2,1)S(1)} %collective-permute-done.7), channel_id=1, source_target_pairs={{0,7},{1,0},{2,1},{3,2},{4,3},{5,4},{6,5},{7,6},{8,15},{9,8},{10,9... | collective-permute-start | bytes 884744 | tf_op jit(solution)/shard_map/ppermute | solution.py:18
  216.7 7.0 %collective-permute-start.10 = (bf16[3,24,2048]{2,1,0:T(8,128)(2,1)S(1)}, bf16[3,24,2048]{2,1,0:T(8,128)(2,1)S(1)}, u32[]{:S(2)}, u32[]{:S(2)}) collective-permute-start(bf16[3,24,2048]{2,1,0:T(8,128)(2,1)S(1)} %collective-permute-done.8), channel_id=1, source_target_pairs={{0,1},{1,2},{2,3},{3,4},{4,5},{5,6},{6,7},{7,0},{8,9},{9,10},{10,1... | collective-permute-start | bytes 884744 | tf_op jit(solution)/shard_map/ppermute | solution.py:15
  226.9 33.6 %all-to-all-start.2 = ((f32[8,3,12]{2,1,0:T(4,128)}), f32[8,3,12]{2,1,0:T(4,128)S(1)}, u32[]{:S(2)}, u32[]{:S(2)}) async-start(f32[8,3,12]{2,1,0:T(4,128)} %all_to_all.26), calls=%async_computation.2 | async-start | bytes 32768 | tf_op jit(solution)/shard_map/all_to_all | solution.py:137
  239.6 5.0 %copy-start.2 = (bf16[24,64,32]{2,1,0:T(8,128)(2,1)S(1)}, bf16[24,64,32]{2,1,0:T(8,128)(2,1)}, u32[]{:S(2)}) copy-start(bf16[24,64,32]{2,1,0:T(8,128)(2,1)} %reshape.48) | copy-start | bytes 294916
  260.5 16.7 %all-to-all-start.3 = ((f32[24,7,1024]{2,1,0:T(8,128)}), f32[24,7,1024]{2,1,0:T(8,128)S(1)}, u32[]{:S(2)}, u32[]{:S(2)}) async-start(f32[24,7,1024]{2,1,0:T(8,128)} %scatter_fusion.1), calls=%async_computation.3 | async-start | bytes 1572864 | tf_op jit(solution)/shard_map/all_to_all | solution.py:136
